TPU v7x, 32 devices: a whole 2x2x4 slice. The times are simulated.
32 devices in a mesh: node: 8 (over z, core), local: 4 (over y, x).
Axes of the slice: x: 2, y: 2, z: 4, core: 2. Of those that a mesh axis runs over, the one named last changes fastest.
Arguments:
- tokens: bfloat16 [256, 3584], P(('node', 'local')), may hold values from -6 to 6
- expert_ids: int32 [256, 4], P(('node', 'local')), may hold values from 0 to 31, as said below
- combine_codes: int32 [256, 4], P(('node', 'local')), may hold values from 1 to 16
- gate_weight: bfloat16 [32, 3584, 1024], P(('node', 'local')), may hold values from -0.09375 to 0.09375
- up_weight: bfloat16 [32, 3584, 1024], P(('node', 'local')), may hold values from -0.09375 to 0.09375
- down_weight: bfloat16 [32, 1024, 3584], P(('node', 'local')), may hold values from -0.1875 to 0.1875
Outputs:
- moe_out: bfloat16 [256, 3584], P(('node', 'local'))
Inputs may be any that keep to these rules, and one draw needn't show every extreme that they name: `expert_ids`: expert e belongs to node group e // 4. A token never names two experts of one node group. The 4 ids of each block of 8 rows (the rows of one device) name every node group exactly 4 times. Over all rows r with one value of (r // 8) % 4, no expert is named more than 16 times, and in every node group some expert is named exactly that often.
All inputs are finite; a program needn't handle non-finite values.
Results may differ from a plain program's by a relative error of at most 0.011.
Values may be sent and summed in bfloat16 or wider, within the bound.
A program may use at most 64 MiB of HBM per device.

v0:
```python
import jax
import jax.numpy as jnp
from jax import lax
from jax.sharding import PartitionSpec as P

TOP = 4
EXP_NODE = 4


def rank_within(labels, count):
    marks = (labels[:, None] == jnp.arange(count, dtype=jnp.int32)[None, :]).astype(jnp.int32)
    before = jnp.cumsum(marks, axis=0) - marks
    return jnp.sum(before * marks, axis=1)


def onehot_rows(targets, count):
    return targets[None, :] == jnp.arange(count, dtype=jnp.int32)[:, None]


def body(tokens, expert_ids, combine_codes, gate_weight, up_weight, down_weight):
    node_count = lax.axis_size("node")
    local_count = lax.axis_size("local")
    experts_here = EXP_NODE
    slices = local_count // experts_here
    token_count, width = tokens.shape
    route_count = token_count * TOP
    per_node = route_count // node_count
    capacity = min(route_count, 2 * route_count // experts_here)
    flat_ids = expert_ids.reshape(route_count)
    target_node = flat_ids // experts_here
    member = flat_ids % experts_here
    slot = target_node * per_node + rank_within(target_node, node_count)
    select = onehot_rows(slot, route_count)
    route_token = jnp.arange(route_count, dtype=jnp.int32) // TOP
    slot_token = jnp.sum(jnp.where(select, route_token[None, :], 0), axis=1)
    slot_member = jnp.sum(jnp.where(select, member[None, :], 0), axis=1)
    pick = (slot_token[:, None] == jnp.arange(token_count, dtype=jnp.int32)[None, :]).astype(
        jnp.bfloat16
    )
    outgoing = jnp.dot(pick, tokens, preferred_element_type=jnp.float32).astype(jnp.bfloat16)
    outgoing = outgoing.reshape(node_count, per_node, width)
    arrived, arrived_member = (
        lax.all_to_all(outgoing, "node", split_axis=0, concat_axis=0, tiled=True),
        lax.all_to_all(
            slot_member.reshape(node_count, per_node),
            "node",
            split_axis=0,
            concat_axis=0,
            tiled=True,
        ),
    )
    arrived = arrived.reshape(route_count, width)
    arrived_member = arrived_member.reshape(route_count)
    place_slot = arrived_member * capacity + rank_within(arrived_member, experts_here)
    place = onehot_rows(place_slot, experts_here * capacity).astype(jnp.bfloat16)
    bundle = jnp.dot(place, arrived, preferred_element_type=jnp.float32).astype(jnp.bfloat16)
    bundle = bundle.reshape(experts_here, 1, capacity, width)
    forward_rows = jnp.broadcast_to(bundle, (experts_here, slices, capacity, width)).reshape(
        local_count, capacity, width
    )
    rows = lax.all_to_all(forward_rows, "local", split_axis=0, concat_axis=0, tiled=True)
    row_shape = rows.shape
    flat_rows = rows.reshape(-1, width)
    gate = jnp.dot(flat_rows, gate_weight[0], preferred_element_type=jnp.float32)
    upper = jnp.dot(flat_rows, up_weight[0], preferred_element_type=jnp.float32)
    hidden = (jax.nn.silu(gate) * upper).astype(jnp.bfloat16)
    projected = jnp.dot(hidden, down_weight[0], preferred_element_type=jnp.float32)
    partial_out = projected.astype(jnp.bfloat16).reshape(row_shape)
    returned = lax.all_to_all(partial_out, "local", split_axis=0, concat_axis=0, tiled=True)
    summed = jnp.sum(
        returned.astype(jnp.float32).reshape(experts_here, slices, capacity, width), axis=1
    )
    summed = summed.astype(jnp.bfloat16)
    results = jnp.dot(
        place.T, summed.reshape(experts_here * capacity, width), preferred_element_type=jnp.float32
    )
    results = results.astype(jnp.bfloat16).reshape(node_count, per_node, width)
    home = lax.all_to_all(results, "node", split_axis=0, concat_axis=0, tiled=True).reshape(
        route_count, width
    )
    route_out = jnp.dot(select.T.astype(jnp.bfloat16), home, preferred_element_type=jnp.float32)
    codes = combine_codes.astype(jnp.float32)
    weights = codes / jnp.sum(codes, axis=1, keepdims=True)
    mixed = jnp.sum(weights[:, :, None] * route_out.reshape(token_count, TOP, width), axis=1)
    return mixed.astype(jnp.bfloat16)


def solution(mesh):
    in_specs = (
        P(("node", "local"), None),
        P(("node", "local"), None),
        P(("node", "local"), None),
        P(("node", "local"), None, None),
        P(("node", "local"), None, None),
        P(("node", "local"), None, None),
    )
    out_specs = P(("node", "local"), None)
    return jax.shard_map(body, mesh=mesh, in_specs=in_specs, out_specs=out_specs, check_vma=False)
```

profile of v0, /device:TPU:0, one launch (start us, length us, event | category | flops | bytes accessed | tf_op | source)
XLA Modules:
  0.0 74.8 jit_solution(11107461722966132042)
XLA Ops:
  0.0 0.8 %copy.26 = s32[8,4]{1,0:T(8,128)S(1)} copy(s32[8,4]{0,1:T(4,128)} %param.7) | data formatting | bytes 256 | tf_op args[1]
  0.8 0.1 reshape.161
  0.9 0.1 fusion.27
  1.0 0.2 select_reduce_fusion.3
  1.2 0.1 select_reduce_fusion.2
  1.3 0.7 all_to_all.18
  2.0 6.4 %all-to-all-start = ((s32[8,1,4]{2,1,0:T(1,128)}), s32[8,1,4]{2,1,0:T(1,128)S(1)}, u32[]{:S(2)}, u32[]{:S(2)}) async-start(s32[8,1,4]{2,1,0:T(1,128)} %bitcast.1), calls=%async_computation | async-start | bytes 8192 | tf_op jit(solution)/shard_map/all_to_all | solution.py:44
  8.3 0.3 convolution_convert_fusion.2
  8.6 0.7 reshape.163
  9.3 4.5 %all-to-all-done = s32[8,1,4]{2,1,0:T(1,128)S(1)} async-done(((s32[8,1,4]{2,1,0:T(1,128)}), s32[8,1,4]{2,1,0:T(1,128)S(1)}, u32[]{:S(2)}, u32[]{:S(2)}) %all-to-all-start) | async-done | bytes 160 | tf_op jit(solution)/shard_map/all_to_all | solution.py:44
  13.9 3.4 %all-to-all-start.1 = ((bf16[8,4,3584]{2,1,0:T(4,128)(2,1)}), bf16[8,4,3584]{2,1,0:T(4,128)(2,1)S(1)}, u32[]{:S(2)}, u32[]{:S(2)}) async-start(bf16[8,4,3584]{2,1,0:T(4,128)(2,1)} %reshape.163), calls=%async_computation.1 | async-start | bytes 458752 | tf_op jit(solution)/shard_map/all_to_all | solution.py:43
  17.3 0.5 broadcast.172
  17.8 0.7 reduce.3
  18.4 0.1 reshape.162
  18.5 0.1 fusion.26
  18.7 0.2 select_reduce_fusion.1
  18.9 7.3 %all-to-all-done.1 = bf16[8,4,3584]{2,1,0:T(4,128)(2,1)S(1)} async-done(((bf16[8,4,3584]{2,1,0:T(4,128)(2,1)}), bf16[8,4,3584]{2,1,0:T(4,128)(2,1)S(1)}, u32[]{:S(2)}, u32[]{:S(2)}) %all-to-all-start.1) | async-done | bytes 229408 | tf_op jit(solution)/shard_map/all_to_all | solution.py:43
  26.2 0.1 reshape.164
  26.3 0.3 convolution_convert_fusion
  26.5 11.2 %all_to_all.29 = bf16[4,16,3584]{2,1,0:T(8,128)(2,1)S(1)} all-to-all(bf16[4,16,3584]{2,1,0:T(8,128)(2,1)S(1)} %bitcast.34), channel_id=1, replica_groups=mesh['node'=8,'local'=4] {'local'}, dimensions={0} | all-to-all | bytes 917504 | tf_op jit(solution)/shard_map/all_to_all | solution.py:61
  37.7 4.5 %fusion.4 = f32[64,1024]{1,0:T(8,128)S(1)} fusion(bf16[64,3584]{1,0:T(8,128)(2,1)S(1)} %bitcast.31, bf16[1,3584,1024]{2,1,0:T(8,128)(2,1)} %param.9), kind=kOutput, calls=%fused_computation.4 | convolution fusion | flops 469762048 | bytes 8060928 | tf_op jit(solution)/shard_map/dot_general | solution.py:64
  42.2 8.6 %fusion.6 = bf16[64,3584]{1,0:T(8,128)(2,1)} fusion(bf16[1,1024,3584]{2,1,0:T(8,128)(2,1)} %param.11, bf16[64,3584]{1,0:T(8,128)(2,1)S(1)} %bitcast.32, bf16[1,3584,1024]{2,1,0:T(8,128)(2,1)} %param.10, f32[64,1024]{1,0:T(8,128)S(1)} %fusion.4), kind=kOutput, calls=%fused_computation.7 | convolution fusion | flops 940146688 | bytes 15859712 | tf_op jit(solution)/shard_map/dot_general | solution.py:67
  50.8 3.5 %all-to-all-start.3 = ((bf16[4,16,3584]{2,1,0:T(8,128)(2,1)}), bf16[4,16,3584]{2,1,0:T(8,128)(2,1)S(1)}, u32[]{:S(2)}, u32[]{:S(2)}) async-start(bf16[4,16,3584]{2,1,0:T(8,128)(2,1)} %bitcast.7), calls=%async_computation.3 | async-start | bytes 917504 | tf_op jit(solution)/shard_map/all_to_all | solution.py:69
  54.3 0.1 reduce_sum.62
  54.4 6.1 %all-to-all-done.3 = bf16[4,16,3584]{2,1,0:T(8,128)(2,1)S(1)} async-done(((bf16[4,16,3584]{2,1,0:T(8,128)(2,1)}), bf16[4,16,3584]{2,1,0:T(8,128)(2,1)S(1)}, u32[]{:S(2)}, u32[]{:S(2)}) %all-to-all-start.3) | async-done | bytes 458784 | tf_op jit(solution)/shard_map/all_to_all | solution.py:69
  60.5 0.3 convolution_convert_fusion.1
  60.8 0.7 reshape.167
  61.5 3.4 %all-to-all-start.4 = ((bf16[8,4,3584]{2,1,0:T(4,128)(2,1)}), bf16[8,4,3584]{2,1,0:T(4,128)(2,1)S(1)}, u32[]{:S(2)}, u32[]{:S(2)}) async-start(bf16[8,4,3584]{2,1,0:T(4,128)(2,1)} %reshape.167), calls=%async_computation.4 | async-start | bytes 458752 | tf_op jit(solution)/shard_map/all_to_all | solution.py:78
  64.9 0.1 copy.31
  65.0 8.8 %all-to-all-done.4 = bf16[8,4,3584]{2,1,0:T(4,128)(2,1)S(1)} async-done(((bf16[8,4,3584]{2,1,0:T(4,128)(2,1)}), bf16[8,4,3584]{2,1,0:T(4,128)(2,1)S(1)}, u32[]{:S(2)}, u32[]{:S(2)}) %all-to-all-start.4) | async-done | bytes 229408 | tf_op jit(solution)/shard_map/all_to_all | solution.py:78
  73.8 0.1 reshape.169
  73.9 0.9 %fusion.9 = bf16[8,3584]{1,0:T(8,128)(2,1)} fusion(bf16[32,3584,1]{1,0,2:T(8,128)(2,1)S(1)} %reshape.169, f32[8,4]{0,1:T(4,128)S(1)} %convert_divide_fusion, s32[8,4]{0,1:T(4,128)S(1)} %copy.31), kind=kOutput, calls=%fused_computation.11 | convolution fusion | flops 7541760 | bytes 286976 | tf_op jit(solution)/shard_map/dot_general | solution.py:81
  (12 shorter events, 0.2 us)
Async XLA Ops:
  0.0 8.3 %copy-start = (bf16[8,3584]{1,0:T(8,128)(2,1)S(1)}, bf16[8,3584]{1,0:T(8,128)(2,1)}, u32[]{:S(2)}) copy-start(bf16[8,3584]{1,0:T(8,128)(2,1)} %param.6) | copy-start | bytes 172036
  2.0 11.9 %all-to-all-start = ((s32[8,1,4]{2,1,0:T(1,128)}), s32[8,1,4]{2,1,0:T(1,128)S(1)}, u32[]{:S(2)}, u32[]{:S(2)}) async-start(s32[8,1,4]{2,1,0:T(1,128)} %bitcast.1), calls=%async_computation | async-start | bytes 8192 | tf_op jit(solution)/shard_map/all_to_all | solution.py:44
  13.9 12.3 %all-to-all-start.1 = ((bf16[8,4,3584]{2,1,0:T(4,128)(2,1)}), bf16[8,4,3584]{2,1,0:T(4,128)(2,1)S(1)}, u32[]{:S(2)}, u32[]{:S(2)}) async-start(bf16[8,4,3584]{2,1,0:T(4,128)(2,1)} %reshape.163), calls=%async_computation.1 | async-start | bytes 458752 | tf_op jit(solution)/shard_map/all_to_all | solution.py:43
  42.2 22.8 %copy-start.1 = (s32[8,4]{0,1:T(4,128)S(1)}, s32[8,4]{0,1:T(4,128)}, u32[]{:S(2)}) copy-start(s32[8,4]{0,1:T(4,128)} %param.8) | copy-start | bytes 388
  50.8 9.7 %all-to-all-start.3 = ((bf16[4,16,3584]{2,1,0:T(8,128)(2,1)}), bf16[4,16,3584]{2,1,0:T(8,128)(2,1)S(1)}, u32[]{:S(2)}, u32[]{:S(2)}) async-start(bf16[4,16,3584]{2,1,0:T(8,128)(2,1)} %bitcast.7), calls=%async_computation.3 | async-start | bytes 917504 | tf_op jit(solution)/shard_map/all_to_all | solution.py:69
  61.5 12.3 %all-to-all-start.4 = ((bf16[8,4,3584]{2,1,0:T(4,128)(2,1)}), bf16[8,4,3584]{2,1,0:T(4,128)(2,1)S(1)}, u32[]{:S(2)}, u32[]{:S(2)}) async-start(bf16[8,4,3584]{2,1,0:T(4,128)(2,1)} %reshape.167), calls=%async_computation.4 | async-start | bytes 458752 | tf_op jit(solution)/shard_map/all_to_all | solution.py:78
where the time goes:
time: 75.3 us; the launch traced here: 74.8 us
  waiting for transfers between devices  26.8 us (36%)
  starting transfers between devices  16.6 us (22%)
  matrix products  14.8 us (20%)
  blocking collectives  11.2 us (15%)
  local copies, waits for them, and re-layouts  3.88 us (5%)
  other arithmetic  1.46 us (2%)
    all_to_all x1, blocking collectives, body(): lax.all_to_all(forward_rows, 'local', split_axis=0, concat_axis=0, tiled=...  11.2 us
    all_to_all x1, waiting for transfers between devices, body(): lax.all_to_all(results, 'node', split_axis=0, concat_axis=0, tiled=True)  8.8 us
    dot_general x1, matrix products, body(): jnp.dot(hidden, down_weight[0], preferred_element_type=jnp.float32)  8.64 us
    all_to_all x1, waiting for transfers between devices, body(): lax.all_to_all(outgoing, 'node', split_axis=0, concat_axis=0, tiled=True)  7.35 us
    all_to_all x1, starting transfers between devices, body(): lax.all_to_all(slot_member.reshape(node_count, per_node), 'node', split_a...  6.35 us
    all_to_all x1, waiting for transfers between devices, body(): lax.all_to_all(partial_out, 'local', split_axis=0, concat_axis=0, tiled=T...  6.12 us
    all_to_all x1, waiting for transfers between devices, body(): lax.all_to_all(slot_member.reshape(node_count, per_node), 'node', split_a...  4.51 us
    dot_general x1, matrix products, body(): jnp.dot(flat_rows, gate_weight[0], preferred_element_type=jnp.float32)  4.46 us
  transfers between devices with their start and end apart: 4, of which 4 were waited for; matrix products, arithmetic and copies ran while one was open for 4% of the time, Pallas kernels for 0%

commit v1 on v0

v1 whole, which is shorter than its diff:
```python
import functools

import jax
import jax.numpy as jnp
from jax import lax
from jax.experimental import pallas as pl
from jax.experimental.pallas import tpu as pltpu
from jax.sharding import PartitionSpec as P

MESH = pl.DeviceIdType.MESH
TOP = 4
EXP_NODE = 4
SUB = 8
LAG_IN = 2
LAG_RELAY = 2
LAG_HOME = 3
CHUNKS = 7


def plan(width, per_node):
    chunks = CHUNKS if width % (CHUNKS * 128) == 0 else 1
    chunk = width // chunks
    split = 1
    while per_node * split * 2 <= SUB and chunk % (128 * split * 2) == 0:
        split *= 2
    return chunks, chunk, split


def bf(x):
    return x.astype(jnp.bfloat16)


def dot(a, b):
    return jnp.dot(a, b, preferred_element_type=jnp.float32)


def iota(shape, axis):
    return lax.broadcasted_iota(jnp.int32, shape, axis)


def kernel(
    dims,
    tok_hbm, ids_hbm, codes_hbm, gate_hbm, up_hbm, down_hbm,
    out_ref,
    tok, ids_ref, codes_ref, wg, wu, wd,
    meta_out, meta_in, sel_t, w_hi, w_lo, place, pack,
    msg, arrived, bundle, rows, acc_g, acc_u, hidden, part, back, home_out, home,
    in_sem, w_sem, meta_sem, a_send, a_recv, b_send, b_recv, c_send, c_recv, d_send, d_recv,
):
    nodes, locals_, per_node, cap, chunks, chunk, split = dims
    slices = locals_ // EXP_NODE
    slots = EXP_NODE * cap
    lanes = nodes * SUB
    wide = max(lanes, 128)
    piece = chunk // split
    tokens = tok.shape[1]
    me = lax.axis_index("node")
    my = lax.axis_index("local")

    def small(i, src, dst):
        return pltpu.make_async_copy(src, dst, in_sem.at[i])

    smalls = [small(0, ids_hbm, ids_ref), small(1, codes_hbm, codes_ref)]
    for c in range(chunks):
        smalls.append(small(2 + c, tok_hbm.at[:, pl.ds(c * chunk, chunk)], tok.at[c]))
    for copy in smalls:
        copy.start()

    def w_copy(which, c):
        if which == 2:
            return pltpu.make_async_copy(
                down_hbm.at[0, :, pl.ds(pl.multiple_of(c * chunk, 128), chunk)],
                wd.at[c], w_sem.at[2, c])
        src, dst = ((gate_hbm, wg), (up_hbm, wu))[which]
        return pltpu.make_async_copy(
            src.at[0, pl.ds(pl.multiple_of(c * chunk, 128), chunk), :], dst.at[c],
            w_sem.at[which, c])

    for c in range(chunks):
        w_copy(0, c).start()
        w_copy(1, c).start()
    for c in range(chunks):
        w_copy(2, c).start()

    barrier = pltpu.get_barrier_semaphore()

    def node_peer(d):
        return lax.rem(me + d, nodes)

    def local_peer(d):
        return lax.rem(my + d, locals_)

    @pl.loop(1, nodes)
    def _(d):
        pl.semaphore_signal(barrier, inc=1, device_id=(node_peer(d), my), device_id_type=MESH)

    @pl.loop(1, locals_)
    def _(d):
        pl.semaphore_signal(barrier, inc=1, device_id=(me, local_peer(d)), device_id_type=MESH)

    smalls[0].wait()
    smalls[1].wait()
    ids = ids_ref[...]
    codes = codes_ref[...].astype(jnp.float32)
    code_sum = jnp.sum(codes, axis=1, keepdims=True)
    lane = iota((tokens, 128), 1)
    groups = [lax.div(ids[:, k:k + 1], EXP_NODE) for k in range(TOP)]
    valid = jnp.zeros((tokens, 128), jnp.float32)
    for k in range(TOP):
        valid += jnp.where(lane == groups[k], 1.0, 0.0)
    below = jnp.where(iota((tokens, tokens), 0) > iota((tokens, tokens), 1), 1.0, 0.0)
    rank = dot(below, valid)
    wide_lane = iota((tokens, wide), 1)
    sel = [jnp.zeros((tokens, wide), jnp.float32) for _ in range(split)]
    weight = [jnp.zeros((tokens, wide), jnp.float32) for _ in range(split)]
    member_at = jnp.zeros((tokens, wide), jnp.float32)
    for k in range(TOP):
        rank_k = jnp.sum(jnp.where(lane == groups[k], rank, 0.0), axis=1, keepdims=True)
        spot = groups[k] * SUB + rank_k.astype(jnp.int32)
        member = lax.rem(ids[:, k:k + 1], EXP_NODE).astype(jnp.float32) + 1.0
        share = codes[:, k:k + 1] / code_sum
        for j in range(split):
            hit = wide_lane == spot + j * per_node
            sel[j] = sel[j] + jnp.where(hit, 1.0, 0.0)
            weight[j] = weight[j] + jnp.where(hit, share, 0.0)
            member_at = member_at + jnp.where(hit, member, 0.0)
    for j in range(split):
        sel_t[j] = bf(jnp.transpose(sel[j])[:lanes, :])
        high = bf(weight[j][:, :lanes])
        w_hi[j] = high
        w_lo[j] = bf(weight[j][:, :lanes] - high.astype(jnp.float32))
    member_col = jnp.sum(jnp.transpose(member_at), axis=1, keepdims=True)[:lanes]
    meta_out[...] = jnp.broadcast_to(member_col, (lanes, 128)).astype(jnp.int32).reshape(
        nodes, SUB, 128)
    meta_in[me] = meta_out[me]

    pl.semaphore_wait(barrier, nodes + locals_ - 2)

    def node_send(src, dst, s_sem, r_sem):
        @pl.loop(1, nodes)
        def _(d):
            peer = node_peer(d)
            pltpu.make_async_remote_copy(
                src_ref=src.at[peer], dst_ref=dst.at[me], send_sem=s_sem, recv_sem=r_sem,
                device_id=(peer, my), device_id_type=MESH).start()

    def local_send(src, dst, s_sem, r_sem, per):
        for d in range(1, locals_):
            peer = local_peer(d)
            pltpu.make_async_remote_copy(
                src_ref=src.at[lax.div(peer, per)], dst_ref=dst.at[my], send_sem=s_sem,
                recv_sem=r_sem, device_id=(me, peer), device_id_type=MESH).start()

    def drain(ref, count, sem):
        whole = ref.at[pl.ds(0, count)]
        pltpu.make_async_copy(whole, whole, sem).wait()

    node_send(meta_out, meta_in, meta_sem.at[0], meta_sem.at[1])

    for c in range(chunks):
        smalls[2 + c].wait()

    @pl.loop(0, chunks)
    def _(c):
        total = dot(sel_t[0], tok[c, :, 0:piece])
        for j in range(1, split):
            total += dot(sel_t[j], tok[c, :, j * piece:(j + 1) * piece])
        msg[c] = bf(total.reshape(nodes, SUB, piece))
        arrived[c, me] = msg[c, me]
        node_send(msg.at[c], arrived.at[c], a_send.at[c], a_recv.at[c])

    drain(meta_in, nodes - 1, meta_sem.at[1])
    members = meta_in[...].reshape(lanes, 128)
    lane = iota((lanes, 128), 1)
    row = iota((lanes, 128), 0)
    under = bf(jnp.where(iota((lanes, lanes), 0) > iota((lanes, lanes), 1), 1.0, 0.0))
    for j in range(split):
        inside = lax.div(lax.rem(row, SUB), per_node) == j
        mine = jnp.where(inside, members, 0)
        marks = jnp.where(mine == lane + 1, 1.0, 0.0)
        before = dot(under, bf(marks))
        spot = jnp.sum(before * marks, axis=1, keepdims=True).astype(jnp.int32)
        target = jnp.where(mine > 0, (mine - 1) * cap + spot, -1)
        placed = jnp.where(lane == target, 1.0, 0.0)
        place[j] = bf(placed[:, :slots])
        pack[j] = bf(jnp.transpose(placed)[:slots, :])

    acc_g[...] = jnp.zeros_like(acc_g)
    acc_u[...] = jnp.zeros_like(acc_u)

    @pl.loop(0, chunks + LAG_IN)
    def _(step):
        @pl.when(step < chunks)
        def _():
            c = step
            drain(arrived.at[c], nodes - 1, a_recv.at[c])
            got = arrived[c].reshape(lanes, piece)
            for j in range(split):
                bundle[c, :, :, j * piece:(j + 1) * piece] = bf(
                    dot(pack[j], got).reshape(EXP_NODE, cap, piece))
            rows[c, my] = bundle[c, lax.div(my, slices)]
            local_send(bundle.at[c], rows.at[c], b_send.at[c], b_recv.at[c], slices)

        @pl.when(step >= LAG_IN)
        def _():
            c = step - LAG_IN
            w_copy(0, c).wait()
            w_copy(1, c).wait()
            drain(rows.at[c], locals_ - 1, b_recv.at[c])
            x = rows[c].reshape(locals_ * cap, chunk)
            acc_g[...] += dot(x, wg[c])
            acc_u[...] += dot(x, wu[c])

    gate = acc_g[...]
    hidden[...] = bf(gate / (1.0 + jnp.exp(-gate)) * acc_u[...])

    @pl.loop(0, chunks + LAG_RELAY + LAG_HOME)
    def _(step):
        @pl.when(step < chunks)
        def _():
            c = step
            w_copy(2, c).wait()
            part[c] = bf(dot(hidden[...], wd[c]).reshape(locals_, cap, chunk))
            back[c, my] = part[c, my]
            local_send(part.at[c], back.at[c], c_send.at[c], c_recv.at[c], 1)

        @pl.when((step >= LAG_RELAY) & (step < chunks + LAG_RELAY))
        def _():
            c = step - LAG_RELAY
            drain(back.at[c], locals_ - 1, c_recv.at[c])
            if slices == 1:
                got = back[c].reshape(slots, chunk)
            else:
                got = bf(jnp.sum(
                    back[c].astype(jnp.float32).reshape(EXP_NODE, slices, cap, chunk),
                    axis=1)).reshape(slots, chunk)
            total = dot(place[0], got[:, 0:piece])
            for j in range(1, split):
                total += dot(place[j], got[:, j * piece:(j + 1) * piece])
            home_out[c] = bf(total.reshape(nodes, SUB, piece))
            home[c, me] = home_out[c, me]
            node_send(home_out.at[c], home.at[c], d_send.at[c], d_recv.at[c])

        @pl.when(step >= LAG_RELAY + LAG_HOME)
        def _():
            c = step - LAG_RELAY - LAG_HOME
            drain(home.at[c], nodes - 1, d_recv.at[c])
            got = home[c].reshape(lanes, piece)
            for j in range(split):
                value = dot(w_hi[j], got) + dot(w_lo[j], got)
                at = pl.multiple_of(c * chunk + j * piece, 128)
                out_ref[:, pl.ds(at, piece)] = bf(value)

    drain(meta_out, nodes - 1, meta_sem.at[0])

    @pl.loop(0, chunks)
    def _(c):
        drain(msg.at[c], nodes - 1, a_send.at[c])
        drain(rows.at[c], locals_ - 1, b_send.at[c])
        drain(part.at[c], locals_ - 1, c_send.at[c])
        drain(home_out.at[c], nodes - 1, d_send.at[c])


def body(tokens, expert_ids, combine_codes, gate_weight, up_weight, down_weight):
    nodes = lax.axis_size("node")
    locals_ = lax.axis_size("local")
    count, width = tokens.shape
    hid = gate_weight.shape[2]
    routes = count * TOP
    per_node = routes // nodes
    cap = min(routes, 2 * routes // EXP_NODE)
    chunks, chunk, split = plan(width, per_node)
    piece = chunk // split
    lanes = nodes * SUB
    slots = EXP_NODE * cap
    many = locals_ * cap
    b16, f32, i32 = jnp.bfloat16, jnp.float32, jnp.int32
    dims = (nodes, locals_, per_node, cap, chunks, chunk, split)
    dma = pltpu.SemaphoreType.DMA
    return pl.pallas_call(
        functools.partial(kernel, dims),
        out_shape=jax.ShapeDtypeStruct((count, width), b16),
        in_specs=[pl.BlockSpec(memory_space=pl.ANY)] * 6,
        out_specs=pl.BlockSpec(memory_space=pltpu.VMEM),
        scratch_shapes=[
            pltpu.VMEM((chunks, count, chunk), b16),
            pltpu.VMEM((count, TOP), i32),
            pltpu.VMEM((count, TOP), i32),
            pltpu.VMEM((chunks, chunk, hid), b16),
            pltpu.VMEM((chunks, chunk, hid), b16),
            pltpu.VMEM((chunks, hid, chunk), b16),
            pltpu.VMEM((nodes, SUB, 128), i32),
            pltpu.VMEM((nodes, SUB, 128), i32),
            pltpu.VMEM((split, lanes, count), b16),
            pltpu.VMEM((split, count, lanes), b16),
            pltpu.VMEM((split, count, lanes), b16),
            pltpu.VMEM((split, lanes, slots), b16),
            pltpu.VMEM((split, slots, lanes), b16),
            pltpu.VMEM((chunks, nodes, SUB, piece), b16),
            pltpu.VMEM((chunks, nodes, SUB, piece), b16),
            pltpu.VMEM((chunks, EXP_NODE, cap, chunk), b16),
            pltpu.VMEM((chunks, locals_, cap, chunk), b16),
            pltpu.VMEM((many, hid), f32),
            pltpu.VMEM((many, hid), f32),
            pltpu.VMEM((many, hid), b16),
            pltpu.VMEM((chunks, locals_, cap, chunk), b16),
            pltpu.VMEM((chunks, locals_, cap, chunk), b16),
            pltpu.VMEM((chunks, nodes, SUB, piece), b16),
            pltpu.VMEM((chunks, nodes, SUB, piece), b16),
            dma((2 + chunks,)),
            dma((3, chunks)),
            dma((2,)),
            dma((chunks,)), dma((chunks,)),
            dma((chunks,)), dma((chunks,)),
            dma((chunks,)), dma((chunks,)),
            dma((chunks,)), dma((chunks,)),
        ],
        compiler_params=pltpu.CompilerParams(collective_id=0, has_side_effects=True),
    )(tokens, expert_ids, combine_codes, gate_weight, up_weight, down_weight)


def solution(mesh):
    in_specs = (
        P(("node", "local"), None),
        P(("node", "local"), None),
        P(("node", "local"), None),
        P(("node", "local"), None, None),
        P(("node", "local"), None, None),
        P(("node", "local"), None, None),
    )
    out_specs = P(("node", "local"), None)
    return jax.shard_map(body, mesh=mesh, in_specs=in_specs, out_specs=out_specs, check_vma=False)
```

time: 75.3 us -> 48 us (0.64)
  Pallas kernels: 0 us -> 43.6 us
  waiting for transfers between devices: 26.8 us -> 0 us
  starting transfers between devices: 16.6 us -> 0 us
  matrix products: 14.8 us -> 0 us
  blocking collectives: 11.2 us -> 0 us
  other arithmetic: 1.46 us -> 0 us
    pallas_call x0 -> x1, Pallas kernels: none -> 43.6 us  [body(): pl.pallas_call(functools.partial(kernel, dims), out_shape=jax.ShapeDtypeS...]
    all_to_all x4 -> x0, waiting for transfers between devices: 26.8 us -> none  [the longest x1 8.8 us: body(): lax.all_to_all(results, 'node', split_axis=0, concat_axis=0, tiled=True)]
    all_to_all x4 -> x0, starting transfers between devices: 16.6 us -> none  [the longest x1 6.35 us: body(): lax.all_to_all(slot_member.reshape(node_count, per_node), 'node', split_a...]
    dot_general x6 -> x0, matrix products: 14.8 us -> none  [the longest x1 8.64 us: body(): jnp.dot(hidden, down_weight[0], preferred_element_type=jnp.float32)]
    all_to_all x1 -> x0, blocking collectives: 11.2 us -> none  [body(): lax.all_to_all(forward_rows, 'local', split_axis=0, concat_axis=0, tiled=...]
    unnamed x5 -> x3, local copies, waits for them, and re-layouts: 0.77 us -> 4.14 us
    reshape x6 -> x0, local copies, waits for them, and re-layouts: 1.75 us -> none  [the longest x1 0.74 us: body(): outgoing = outgoing.reshape(node_count, per_node, width)]
    all_to_all x2 -> x0, local copies, waits for them, and re-layouts: 1.2 us -> none  [body(): lax.all_to_all(slot_member.reshape(node_count, per_node), 'node', split_a...]
  transfers between devices with their start and end apart: 4 -> 0, of which waited for: 4 -> 0; matrix products, arithmetic and copies ran while one was open for 4% -> 0% of each run, Pallas kernels for 0% -> 0%
where the time goes in v1:
time: 48 us; the launch traced here: 47.8 us
  Pallas kernels  43.6 us (91%)
  local copies, waits for them, and re-layouts  4.14 us (9%)
    pallas_call x1, Pallas kernels, body(): pl.pallas_call(functools.partial(kernel, dims), out_shape=jax.ShapeDtypeS...  43.6 us
    unnamed x3, local copies, waits for them, and re-layouts  4.14 us

profile of v1, /device:TPU:0, one launch (start us, length us, event | category | flops | bytes accessed | tf_op | source)
XLA Modules:
  0.0 47.8 jit_solution(1218333788037124159)
XLA Ops:
  0.0 1.3 %copy.7.ids_hbm = s32[8,4]{1,0:T(8,128)} copy(s32[8,4]{0,1:T(4,128)} %param.7) | data formatting | bytes 256 | tf_op args[1]
  1.3 1.3 %copy.8.codes_hbm = s32[8,4]{1,0:T(8,128)} copy(s32[8,4]{0,1:T(4,128)} %param.8) | data formatting | bytes 256 | tf_op args[2]
  2.7 43.6 %shard_map.64 = bf16[8,3584]{1,0:T(8,128)(2,1)} custom-call(bf16[8,3584]{1,0:T(8,128)(2,1)} %tok_hbm.1, s32[8,4]{1,0:T(8,128)} %copy.7.ids_hbm, s32[8,4]{1,0:T(8,128)} %copy.8.codes_hbm, bf16[1,3584,1024]{2,1,0:T(8,128)(2,1)} %gate_hbm.1, bf16[1,3584,1024]{2,1,0:T(8,128)(2,1)} %up_hbm.1, bf16[1,1024,3584]{2,1,0:T(8,128)(2,1)} %down_hbm.1), custom_call_target="tpu_custom_call" | custom-call | tf_op jit(solution)/shard_map/pallas_call | solution.py:280
  46.3 1.4 %copy.10 = bf16[8,3584]{1,0:T(8,128)(2,1)} copy(bf16[8,3584]{1,0:T(8,128)(2,1)} %shard_map.64) | data formatting | bytes 114688

commit v2 on v1

v2 whole, which is shorter than its diff:
```python
import functools

import jax
import jax.numpy as jnp
from jax import lax
from jax.experimental import pallas as pl
from jax.experimental.pallas import tpu as pltpu
from jax.sharding import PartitionSpec as P

MESH = pl.DeviceIdType.MESH
TOP = 4
EXP_NODE = 4
SUB = 8
IN_PARTS = (5, 5, 4)
OUT_PARTS = (4, 5, 5)
LAG_IN = 2
LAG_RELAY = 2
LAG_HOME = 2


def cut(units, parts):
    total, seen, edges = sum(parts), 0, [0]
    for part in parts:
        seen += part
        edges.append(units * seen // total)
    return [(a, b - a) for a, b in zip(edges[:-1], edges[1:]) if b > a]


def plan(width, per_node):
    split = 1
    while per_node * split * 2 <= SUB and width % (128 * split * 2) == 0:
        split *= 2
    unit = 128 * split
    scale = lambda spans: [(a * unit, n * unit) for a, n in spans]
    return split, scale(cut(width // unit, IN_PARTS)), scale(cut(width // unit, OUT_PARTS))


def bf(x):
    return x.astype(jnp.bfloat16)


def dot(a, b):
    return jnp.dot(a, b, preferred_element_type=jnp.float32)


def iota(shape, axis):
    return lax.broadcasted_iota(jnp.int32, shape, axis)


def kernel(dims, counts, *refs):
    nodes, locals_, per_node, cap, split, spans_in, spans_out = dims
    refs = iter(refs)
    groups_of = []
    for count in counts:
        taken = [next(refs) for _ in range(max(count, 1))]
        groups_of.append(taken if count else taken[0])
    (tok_hbm, ids_hbm, codes_hbm, gate_hbm, up_hbm, down_hbm, out_ref,
     tok, ids_ref, codes_ref, meta_out, meta_in, sel_t, w_hi, w_lo, place, pack,
     acc_g, acc_u, hidden,
     wg, wu, msg, arrived, bundle, rows,
     wd, part, back, home_out, home,
     in_sem, w_sem, meta_sem, a_send, a_recv, b_send, b_recv,
     c_send, c_recv, d_send, d_recv) = groups_of
    slices = locals_ // EXP_NODE
    slots = EXP_NODE * cap
    lanes = nodes * SUB
    wide = max(lanes, 128)
    tokens = tok.shape[0]
    me = lax.axis_index("node")
    my = lax.axis_index("local")
    n_in, n_out = len(spans_in), len(spans_out)

    smalls = [
        pltpu.make_async_copy(src, dst, in_sem.at[i])
        for i, (src, dst) in enumerate(
            ((ids_hbm, ids_ref), (codes_hbm, codes_ref), (tok_hbm, tok)))
    ]
    for copy in smalls:
        copy.start()

    barrier = pltpu.get_barrier_semaphore()

    def node_peer(d):
        return lax.rem(me + d, nodes)

    def local_peer(d):
        return lax.rem(my + d, locals_)

    @pl.loop(1, nodes)
    def _(d):
        pl.semaphore_signal(barrier, inc=1, device_id=(node_peer(d), my), device_id_type=MESH)

    @pl.loop(1, locals_)
    def _(d):
        pl.semaphore_signal(barrier, inc=1, device_id=(me, local_peer(d)), device_id_type=MESH)

    first = [
        [pltpu.make_async_copy(src.at[0, pl.ds(at, size), :], dst[c], w_sem.at[which, c])
         for which, (src, dst) in enumerate(((gate_hbm, wg), (up_hbm, wu)))]
        for c, (at, size) in enumerate(spans_in)
    ]
    second = [
        pltpu.make_async_copy(down_hbm.at[0, :, pl.ds(at, size)], wd[c], w_sem.at[2, c])
        for c, (at, size) in enumerate(spans_out)
    ]
    for pair in first:
        for copy in pair:
            copy.start()
    for copy in second:
        copy.start()

    smalls[0].wait()
    smalls[1].wait()
    same = iota((tokens, tokens), 0) == iota((tokens, tokens), 1)

    def column(ref, k):
        return jnp.sum(jnp.where(same, ref[k:k + 1, :], 0), axis=1, keepdims=True)

    ids = [column(ids_ref, k) for k in range(TOP)]
    codes = [column(codes_ref, k).astype(jnp.float32) for k in range(TOP)]
    code_sum = sum(codes[1:], codes[0])
    lane = iota((tokens, 128), 1)
    groups = [lax.div(ids[k], EXP_NODE) for k in range(TOP)]
    valid = jnp.zeros((tokens, 128), jnp.float32)
    for k in range(TOP):
        valid += jnp.where(lane == groups[k], 1.0, 0.0)
    below = jnp.where(iota((tokens, tokens), 0) > iota((tokens, tokens), 1), 1.0, 0.0)
    rank = dot(below, valid)
    wide_lane = iota((tokens, wide), 1)
    sel = [jnp.zeros((tokens, wide), jnp.float32) for _ in range(split)]
    weight = [jnp.zeros((tokens, wide), jnp.float32) for _ in range(split)]
    member_at = jnp.zeros((tokens, wide), jnp.float32)
    for k in range(TOP):
        rank_k = jnp.sum(jnp.where(lane == groups[k], rank, 0.0), axis=1, keepdims=True)
        spot = groups[k] * SUB + rank_k.astype(jnp.int32)
        member = lax.rem(ids[k], EXP_NODE).astype(jnp.float32) + 1.0
        share = codes[k] / code_sum
        for j in range(split):
            hit = wide_lane == spot + j * per_node
            sel[j] = sel[j] + jnp.where(hit, 1.0, 0.0)
            weight[j] = weight[j] + jnp.where(hit, share, 0.0)
            member_at = member_at + jnp.where(hit, member, 0.0)
    for j in range(split):
        sel_t[j] = bf(jnp.transpose(sel[j])[:lanes, :])
        high = bf(weight[j][:, :lanes])
        w_hi[j] = high
        w_lo[j] = bf(weight[j][:, :lanes] - high.astype(jnp.float32))
    member_col = jnp.sum(jnp.transpose(member_at), axis=1, keepdims=True)[:lanes]
    meta_out[...] = jnp.broadcast_to(member_col, (lanes, 128)).astype(jnp.int32).reshape(
        nodes, SUB, 128)
    meta_in[me] = meta_out[me]

    def node_send(src, dst, s_sem, r_sem):
        @pl.loop(1, nodes)
        def _(d):
            peer = node_peer(d)
            pltpu.make_async_remote_copy(
                src_ref=src.at[peer], dst_ref=dst.at[me], send_sem=s_sem, recv_sem=r_sem,
                device_id=(peer, my), device_id_type=MESH).start()

    def local_send(src, dst, s_sem, r_sem, per):
        for d in range(1, locals_):
            peer = local_peer(d)
            pltpu.make_async_remote_copy(
                src_ref=src.at[lax.div(peer, per)], dst_ref=dst.at[my], send_sem=s_sem,
                recv_sem=r_sem, device_id=(me, peer), device_id_type=MESH).start()

    def drain(ref, count, sem):
        whole = ref.at[pl.ds(0, count)]
        pltpu.make_async_copy(whole, whole, sem).wait()

    smalls[2].wait()

    def fill_msg(c):
        at, size = spans_in[c]
        piece = size // split
        total = dot(sel_t[0], tok[:, at:at + piece])
        for j in range(1, split):
            total += dot(sel_t[j], tok[:, at + j * piece:at + (j + 1) * piece])
        msg[c][...] = bf(total.reshape(nodes, SUB, piece))
        arrived[c][me] = msg[c][me]

    for c in range(n_in):
        fill_msg(c)
    pl.semaphore_wait(barrier, nodes + locals_ - 2)
    node_send(meta_out, meta_in, meta_sem.at[0], meta_sem.at[1])
    for c in range(n_in):
        node_send(msg[c], arrived[c], a_send.at[c], a_recv.at[c])

    drain(meta_in, nodes - 1, meta_sem.at[1])
    members = meta_in[...].reshape(lanes, 128)
    lane = iota((lanes, 128), 1)
    row = iota((lanes, 128), 0)
    under = bf(jnp.where(iota((lanes, lanes), 0) > iota((lanes, lanes), 1), 1.0, 0.0))
    for j in range(split):
        inside = lax.div(lax.rem(row, SUB), per_node) == j
        mine = jnp.where(inside, members, 0)
        marks = jnp.where(mine == lane + 1, 1.0, 0.0)
        before = dot(under, bf(marks))
        spot = jnp.sum(before * marks, axis=1, keepdims=True).astype(jnp.int32)
        target = jnp.where(mine > 0, (mine - 1) * cap + spot, -1)
        placed = jnp.where(lane == target, 1.0, 0.0)
        place[j] = bf(placed[:, :slots])
        pack[j] = bf(jnp.transpose(placed)[:slots, :])

    def forward(c):
        piece = spans_in[c][1] // split
        drain(arrived[c], nodes - 1, a_recv.at[c])
        got = arrived[c][...].reshape(lanes, piece)
        for j in range(split):
            bundle[c][:, :, j * piece:(j + 1) * piece] = bf(
                dot(pack[j], got).reshape(EXP_NODE, cap, piece))
        rows[c][my] = bundle[c][lax.div(my, slices)]
        local_send(bundle[c], rows[c], b_send.at[c], b_recv.at[c], slices)

    def expand(c):
        first[c][0].wait()
        first[c][1].wait()
        drain(rows[c], locals_ - 1, b_recv.at[c])
        x = rows[c][...].reshape(locals_ * cap, spans_in[c][1])
        if c == 0:
            acc_g[...] = dot(x, wg[c][...])
            acc_u[...] = dot(x, wu[c][...])
        else:
            acc_g[...] += dot(x, wg[c][...])
            acc_u[...] += dot(x, wu[c][...])

    for step in range(n_in + LAG_IN):
        if step < n_in:
            forward(step)
        if step >= LAG_IN:
            expand(step - LAG_IN)

    gate = acc_g[...]
    hidden[...] = bf(gate / (1.0 + jnp.exp(-gate)) * acc_u[...])

    def project(c):
        second[c].wait()
        part[c][...] = bf(dot(hidden[...], wd[c][...]).reshape(locals_, cap, spans_out[c][1]))
        back[c][my] = part[c][my]
        local_send(part[c], back[c], c_send.at[c], c_recv.at[c], 1)

    def relay(c):
        size = spans_out[c][1]
        piece = size // split
        drain(back[c], locals_ - 1, c_recv.at[c])
        if slices == 1:
            got = back[c][...].reshape(slots, size)
        else:
            got = bf(jnp.sum(
                back[c][...].astype(jnp.float32).reshape(EXP_NODE, slices, cap, size),
                axis=1)).reshape(slots, size)
        total = dot(place[0], got[:, 0:piece])
        for j in range(1, split):
            total += dot(place[j], got[:, j * piece:(j + 1) * piece])
        home_out[c][...] = bf(total.reshape(nodes, SUB, piece))
        home[c][me] = home_out[c][me]
        node_send(home_out[c], home[c], d_send.at[c], d_recv.at[c])

    def combine(c):
        at, size = spans_out[c]
        piece = size // split
        drain(home[c], nodes - 1, d_recv.at[c])
        got = home[c][...].reshape(lanes, piece)
        for j in range(split):
            value = dot(w_hi[j], got) + dot(w_lo[j], got)
            out_ref[:, at + j * piece:at + (j + 1) * piece] = bf(value)

    for step in range(n_out + LAG_RELAY + LAG_HOME):
        if step < n_out:
            project(step)
        if LAG_RELAY <= step < n_out + LAG_RELAY:
            relay(step - LAG_RELAY)
        if step >= LAG_RELAY + LAG_HOME:
            combine(step - LAG_RELAY - LAG_HOME)

    drain(meta_out, nodes - 1, meta_sem.at[0])
    for c in range(n_in):
        drain(msg[c], nodes - 1, a_send.at[c])
        drain(rows[c], locals_ - 1, b_send.at[c])
    for c in range(n_out):
        drain(part[c], locals_ - 1, c_send.at[c])
        drain(home_out[c], nodes - 1, d_send.at[c])


def body(tokens, expert_ids, combine_codes, gate_weight, up_weight, down_weight):
    nodes = lax.axis_size("node")
    locals_ = lax.axis_size("local")
    count, width = tokens.shape
    hid = gate_weight.shape[2]
    routes = count * TOP
    per_node = routes // nodes
    cap = min(routes, 2 * routes // EXP_NODE)
    split, spans_in, spans_out = plan(width, per_node)
    lanes = nodes * SUB
    slots = EXP_NODE * cap
    many = locals_ * cap
    b16, f32, i32 = jnp.bfloat16, jnp.float32, jnp.int32
    dims = (nodes, locals_, per_node, cap, split, spans_in, spans_out)
    dma = pltpu.SemaphoreType.DMA
    v = pltpu.VMEM
    most = max(len(spans_in), len(spans_out))
    sizes_in = [n for _, n in spans_in]
    sizes_out = [n for _, n in spans_out]
    scratch = [
        v((count, width), b16), v((TOP, count), i32), v((TOP, count), i32),
        v((nodes, SUB, 128), i32), v((nodes, SUB, 128), i32),
        v((split, lanes, count), b16), v((split, count, lanes), b16),
        v((split, count, lanes), b16),
        v((split, lanes, slots), b16), v((split, slots, lanes), b16),
        v((many, hid), f32), v((many, hid), f32), v((many, hid), b16),
        [v((n, hid), b16) for n in sizes_in],
        [v((n, hid), b16) for n in sizes_in],
        [v((nodes, SUB, n // split), b16) for n in sizes_in],
        [v((nodes, SUB, n // split), b16) for n in sizes_in],
        [v((EXP_NODE, cap, n), b16) for n in sizes_in],
        [v((locals_, cap, n), b16) for n in sizes_in],
        [v((hid, n), b16) for n in sizes_out],
        [v((locals_, cap, n), b16) for n in sizes_out],
        [v((locals_, cap, n), b16) for n in sizes_out],
        [v((nodes, SUB, n // split), b16) for n in sizes_out],
        [v((nodes, SUB, n // split), b16) for n in sizes_out],
        dma((3,)), dma((3, most)), dma((2,)),
    ] + [dma((most,)) for _ in range(8)]
    counts = [0] * 7 + [len(x) if isinstance(x, list) else 0 for x in scratch]
    flat = [y for x in scratch for y in (x if isinstance(x, list) else [x])]
    return pl.pallas_call(
        functools.partial(kernel, dims, counts),
        out_shape=jax.ShapeDtypeStruct((count, width), b16),
        in_specs=[pl.BlockSpec(memory_space=pl.ANY)] * 6,
        out_specs=pl.BlockSpec(memory_space=pltpu.VMEM),
        scratch_shapes=flat,
        compiler_params=pltpu.CompilerParams(collective_id=0, has_side_effects=True),
    )(tokens, expert_ids.T, combine_codes.T, gate_weight, up_weight, down_weight)


def solution(mesh):
    in_specs = (
        P(("node", "local"), None),
        P(("node", "local"), None),
        P(("node", "local"), None),
        P(("node", "local"), None, None),
        P(("node", "local"), None, None),
        P(("node", "local"), None, None),
    )
    out_specs = P(("node", "local"), None)
    return jax.shard_map(body, mesh=mesh, in_specs=in_specs, out_specs=out_specs, check_vma=False)
```

time: 48 us -> 33 us (0.69)
  Pallas kernels: 43.6 us -> 31.4 us
  local copies, waits for them, and re-layouts: 4.14 us -> 1.45 us
    pallas_call x1, Pallas kernels: 43.6 us -> 31.4 us  [body(): pl.pallas_call(functools.partial(kernel, dims, counts), out_shape=jax.Sha...]
    unnamed x3 -> x1, local copies, waits for them, and re-layouts: 4.14 us -> 1.45 us
where the time goes in v2:
time: 33 us; the launch traced here: 32.8 us
  Pallas kernels  31.4 us (95%)
  local copies, waits for them, and re-layouts  1.45 us (4%)
    pallas_call x1, Pallas kernels, body(): pl.pallas_call(functools.partial(kernel, dims, counts), out_shape=jax.Sha...  31.4 us
    unnamed x1, local copies, waits for them, and re-layouts  1.45 us

profile of v2, /device:TPU:0, one launch (start us, length us, event | category | flops | bytes accessed | tf_op | source)
XLA Modules:
  0.0 32.8 jit_solution(4925661699606298485)
XLA Ops:
  0.0 31.4 %shard_map.64 = bf16[8,3584]{1,0:T(8,128)(2,1)} custom-call(bf16[8,3584]{1,0:T(8,128)(2,1)} %refs_0_.1, s32[4,8]{1,0:T(4,128)} %bitcast.2, s32[4,8]{1,0:T(4,128)} %bitcast.3, bf16[1,3584,1024]{2,1,0:T(8,128)(2,1)} %refs_3_.1, bf16[1,3584,1024]{2,1,0:T(8,128)(2,1)} %refs_4_.1, bf16[1,1024,3584]{2,1,0:T(8,128)(2,1)} %refs_5_.1), custom_call_target="tpu_custom_call" | custom-call | tf_op jit(solution)/shard_map/pallas_call | solution.py:327
  31.4 1.4 %copy.8 = bf16[8,3584]{1,0:T(8,128)(2,1)} copy(bf16[8,3584]{1,0:T(8,128)(2,1)} %shard_map.64) | data formatting | bytes 114688

commit v3 on v2

--- a/solution.py
+++ b/solution.py
@@ -11,11 +11,11 @@
 TOP = 4
 EXP_NODE = 4
 SUB = 8
-IN_PARTS = (5, 5, 4)
-OUT_PARTS = (4, 5, 5)
-LAG_IN = 2
-LAG_RELAY = 2
-LAG_HOME = 2
+IN_PARTS = (5, 4, 3, 2)
+OUT_PARTS = (2, 3, 4, 5)
+LAG_IN = 3
+LAG_RELAY = 3
+LAG_HOME = 3
 
 
 def cut(units, parts):
@@ -326,7 +326,7 @@
     flat = [y for x in scratch for y in (x if isinstance(x, list) else [x])]
     return pl.pallas_call(
         functools.partial(kernel, dims, counts),
-        out_shape=jax.ShapeDtypeStruct((count, width), b16),
+        out_shape=pltpu.VMEM((count, width), b16),
         in_specs=[pl.BlockSpec(memory_space=pl.ANY)] * 6,
         out_specs=pl.BlockSpec(memory_space=pltpu.VMEM),
         scratch_shapes=flat,

time: 33 us -> 31.1 us (0.942)
  Pallas kernels: 31.4 us -> 30.3 us
  local copies, waits for them, and re-layouts: 1.45 us -> 0.63 us
    pallas_call x1, Pallas kernels: 31.4 us -> 30.3 us  [body(): pl.pallas_call(functools.partial(kernel, dims, counts), out_shape=pltpu.V...]
    unnamed x1, local copies, waits for them, and re-layouts: 1.45 us -> 0.63 us
where the time goes in v3:
time: 31.1 us; the launch traced here: 30.9 us
  Pallas kernels  30.3 us (97%)
  local copies, waits for them, and re-layouts  0.63 us (2%)
    pallas_call x1, Pallas kernels, body(): pl.pallas_call(functools.partial(kernel, dims, counts), out_shape=pltpu.V...  30.3 us
    unnamed x1, local copies, waits for them, and re-layouts  0.63 us

profile of v3, /device:TPU:0, one launch (start us, length us, event | category | flops | bytes accessed | tf_op | source)
XLA Modules:
  0.0 30.9 jit_solution(2685257308425353481)
XLA Ops:
  0.0 30.3 %shard_map.64 = bf16[8,3584]{1,0:T(8,128)(2,1)S(1)} custom-call(bf16[8,3584]{1,0:T(8,128)(2,1)} %refs_0_.1, s32[4,8]{1,0:T(4,128)} %bitcast.2, s32[4,8]{1,0:T(4,128)} %bitcast.3, bf16[1,3584,1024]{2,1,0:T(8,128)(2,1)} %refs_3_.1, bf16[1,3584,1024]{2,1,0:T(8,128)(2,1)} %refs_4_.1, bf16[1,1024,3584]{2,1,0:T(8,128)(2,1)} %refs_5_.1), custom_call_target="tpu_custom_call" | custom-call | tf_op jit(solution)/shard_map/pallas_call | solution.py:327
  30.3 0.6 %copy.8 = bf16[8,3584]{1,0:T(8,128)(2,1)} copy(bf16[8,3584]{1,0:T(8,128)(2,1)S(1)} %shard_map.64) | data formatting | bytes 114688
